TPU v7x, 512 devices: a whole 4x4x16 slice. The times are simulated.
512 devices in a mesh: mem: 16 (over z_lo, core), lat: 32 (over x, y, z_hi).
Axes of the slice: x: 4, y: 4, z: 16 (z_hi: 2, z_lo: 8; z = z_hi * 8 + z_lo), core: 2. Of those that a mesh axis runs over, the one named last changes fastest.
Arguments:
- control: bfloat16 [32, 10, 704, 1440], P('mem', None, 'lat'), may hold values from -6 to 6
- perturb: bfloat16 [32, 10, 704, 1440], P('mem', None, None, 'lat'), may hold values from -6 to 6
- lon_loc: bfloat16 [1440, 1440], P(None, 'mem'), may hold values from 0 to 1, as said below
- lat_loc: bfloat16 [704, 704], P('mem'), may hold values from 0 to 1, as said below
- static_scale: float32 [10, 704, 1440], P(None, 'mem', 'lat'), may hold values from 0.3 to 1
- static_field: float32 [10, 704, 1440], P(None, 'mem', 'lat'), may hold values from -6 to 6
- courant: float32 [2, 704, 1440], P(None, 'mem', 'lat'), may hold values from -0.48 to 0.48
Outputs:
- increment: float32 [10, 704, 1440], P(None, 'mem', 'lat')
- evolved: float32 [10, 704, 1440], P(None, 'mem', 'lat')
Inputs may be any that keep to these rules, and one draw needn't show every extreme that they name: `lon_loc`: Symmetric, with positive entries. `lat_loc`: Symmetric, with positive entries.
All inputs are finite; a program needn't handle non-finite values.
Results may differ from a plain program's by a relative error of at most 0.0027.
Values may be sent and summed in bfloat16 or wider, within the bound.
A program may use at most 64 MiB of HBM per device.

v0:
```python
import math
import jax
import jax.numpy as jnp
from jax import lax
from jax.sharding import PartitionSpec as P

NLAT = 704
STEPS = 4


def padded_2(shard, sides, width, wrap):
    for axis, dim in sides:
        size, length = (lax.axis_size(axis), shard.shape[dim])
        up = [(i, (i + 1) % size) for i in range(size if wrap else size - 1)]
        down = [(j, i) for i, j in up]
        last = lax.slice_in_dim(shard, length - width, length, axis=dim)
        leading = lax.slice_in_dim(shard, 0, width, axis=dim)
        before = lax.ppermute(last, axis, up)
        after = lax.ppermute(leading, axis, down)
        shard = jnp.concatenate([before, shard, after], axis=dim)
    return shard


def in_order(parts, dim):
    shape = list(parts.shape[1:])
    shape[dim] *= parts.shape[0]
    return jnp.moveaxis(parts, 0, dim).reshape(shape)


def sent_to_all(shard, axis):
    length = lax.axis_size(axis)
    return lax.all_to_all(
        jnp.broadcast_to(shard[None], (length, *shard.shape)), axis, 0, 0, tiled=True
    )


def collect(shard, axis, dim):
    return in_order(sent_to_all(shard, axis), dim)


def upwind(padded, east_west, north_south):
    center = padded[:, 1:-1, 1:-1]
    western = padded[:, 1:-1, :-2]
    eastern = padded[:, 1:-1, 2:]
    southern = padded[:, :-2, 1:-1]
    northern = padded[:, 2:, 1:-1]
    zonal = jnp.maximum(east_west, 0.0) * (center - western) + jnp.minimum(east_west, 0.0) * (
        eastern - center
    )
    meridional = jnp.maximum(north_south, 0.0) * (center - southern) + jnp.minimum(
        north_south, 0.0
    ) * (northern - center)
    return center - zonal - meridional


def lon_rim(values, width):
    return padded_2(values, (("lat", 2),), width, True)


def lat_rim(values, width):
    return padded_2(values, (("mem", 1),), width, False)


def evolve(current, courant):
    fields = current.shape[0]
    stacked = jnp.concatenate([current, courant], axis=0)
    extended = lat_rim(lon_rim(stacked, STEPS), STEPS)
    result = extended[:fields]
    wind_ext = extended[fields:]
    for step_index in range(STEPS):
        margin = step_index + 1
        inner_wind = wind_ext[
            :, margin : wind_ext.shape[1] - margin, margin : wind_ext.shape[2] - margin
        ]
        result = upwind(result, inner_wind[0], inner_wind[1])
    return result


def per_device(control, perturb, lon_loc, lat_loc, static_scale, static_field, courant):
    along_lon = jnp.einsum(
        "mfal,lc->amfc",
        control,
        lax.all_gather(lon_loc, "mem", axis=1, tiled=True),
        preferred_element_type=jnp.float32,
    ).astype(jnp.bfloat16)
    banded = lax.all_to_all(along_lon, "lat", split_axis=3, concat_axis=0, tiled=True)
    mem_here = banded.shape[1]
    fields = banded.shape[2]
    lon_width = banded.shape[3]
    flat_band = banded.reshape(banded.shape[0], mem_here * fields * lon_width)
    pert_rows = jnp.transpose(perturb, (2, 0, 1, 3))
    lat_weights_all = collect(lat_loc, "mem", 0)
    members = mem_here * lax.axis_size("mem")
    ens_scale = 1.0 / math.sqrt(members - 1)
    rows_own = NLAT // lax.axis_size("mem")
    localized = jnp.dot(lat_weights_all, flat_band, preferred_element_type=jnp.float32)
    localized = localized.reshape(NLAT, mem_here, fields, lon_width)
    ensemble_all = jnp.transpose(
        lax.psum(jnp.sum(localized * pert_rows.astype(jnp.float32), axis=1) * ens_scale, "mem"),
        (1, 0, 2),
    )
    offset = lax.axis_index("mem") * rows_own
    ensemble = lax.dynamic_slice_in_dim(ensemble_all, offset, rows_own, 1)
    increment = ensemble + static_scale * static_field
    evolved = evolve(increment, courant)
    return (increment, evolved)


def solution(mesh):
    placed = (
        P("mem", None, "lat", None),
        P("mem", None, None, "lat"),
        P(None, "mem"),
        P("mem", None),
        P(None, "mem", "lat"),
        P(None, "mem", "lat"),
        P(None, "mem", "lat"),
    )
    return jax.shard_map(
        per_device,
        mesh=mesh,
        in_specs=placed,
        out_specs=(P(None, "mem", "lat"), P(None, "mem", "lat")),
        check_vma=False,
    )
```

profile of v0, /device:TPU:1, one launch (start us, length us, event | category | flops | bytes accessed | tf_op | source)
XLA Modules:
  0.0 541.9 jit_solution(11255603198932027136)
XLA Ops:
  7.2 0.7 all-gather.3.cloned.1.call-update
  7.9 2.0 broadcast_in_dim.2
  9.9 14.0 %all-to-all-start.1 = ((bf16[16,44,704]{2,1,0:T(8,128)(2,1)}), bf16[16,44,704]{2,1,0:T(8,128)(2,1)S(1)}, u32[]{:S(2)}, u32[]{:S(2)}) async-start(bf16[16,44,704]{2,1,0:T(8,128)(2,1)} %broadcast_in_dim.2), calls=%async_computation.1 | async-start | bytes 2359296 | tf_op jit(solution)/shard_map/all_to_all | solution.py:32
  23.9 111.8 %all-gather.3.cloned.1.call-done = bf16[16,90,1440]{2,1,0:T(8,128)(2,1)} async-done(((bf16[1,90,1440]{2,1,0:T(8,128)(2,1)}), bf16[16,90,1440]{2,1,0:T(8,128)(2,1)}) %all-gather.3.cloned.1.call-update) | async-done | bytes 4147216 | tf_op jit(solution)/shard_map/all_gather | solution.py:83
  135.8 5.9 %reshape.20 = bf16[1440,1440,1,1]{1,0,2,3:T(8,128)(2,1)} reshape(bf16[16,90,1440]{2,1,0:T(8,128)(2,1)} %all-gather.3.cloned.1.call-done) | data formatting | bytes 8294400
  141.7 6.0 %fusion.6 = bf16[22,2,10,1440]{3,0,2,1:T(8,128)(2,1)} fusion(bf16[1440,1440,1,1]{1,0,2,3:T(8,128)(2,1)} %reshape.20, bf16[2,10,22,1440]{3,0,2,1:T(2,128)(2,1)S(1)} %copy-done), kind=kOutput, calls=%fused_computation.5 | convolution fusion | flops 1825401600 | bytes 6681600 | tf_op jit(solution)/shard_map/mfal,lc->amfc/dot_general | solution.py:80
  147.7 15.6 %copy.36 = bf16[22,2,10,1440]{0,1,2,3:T(2,128)(2,1)} copy(bf16[22,2,10,1440]{3,0,2,1:T(8,128)(2,1)} %fusion.6) | data formatting | bytes 2534400 | tf_op jit(solution)/shard_map/convert_element_type | solution.py:85
  163.3 11.0 %reshape.22 = bf16[32,2,9900]{2,1,0:T(2,128)(2,1)} reshape(bf16[1440,10,2,22]{3,2,1,0:T(2,128)(2,1)} %bitcast.62) | data formatting | bytes 2534400
  174.3 1.0 copy-done.1
  175.3 12.5 %all-to-all-start = ((bf16[32,2,9900]{2,1,0:T(2,128)(2,1)}), bf16[32,2,9900]{2,1,0:T(2,128)(2,1)S(1)}, u32[]{:S(2)}, u32[]{:S(2)}) async-start(bf16[32,2,9900]{2,1,0:T(2,128)(2,1)} %reshape.22), calls=%async_computation | async-start | bytes 2555904 | tf_op jit(solution)/shard_map/all_to_all | solution.py:86
  187.9 2.3 reshape.16
  190.2 44.9 %all-to-all-done = bf16[32,2,9900]{2,1,0:T(2,128)(2,1)S(1)} async-done(((bf16[32,2,9900]{2,1,0:T(2,128)(2,1)}), bf16[32,2,9900]{2,1,0:T(2,128)(2,1)S(1)}, u32[]{:S(2)}, u32[]{:S(2)}) %all-to-all-start) | async-done | bytes 1267232 | tf_op jit(solution)/shard_map/all_to_all | solution.py:86
  235.1 7.4 %reshape.23 = bf16[1440,10,2,22]{3,2,1,0:T(2,128)(2,1)} reshape(bf16[32,2,9900]{2,1,0:T(2,128)(2,1)S(1)} %all-to-all-done) | data formatting | bytes 2534400
  242.5 25.1 %copy.53 = bf16[22,2,10,32,45]{4,2,1,0,3:T(8,128)(2,1)} copy(bf16[22,2,10,32,45]{0,1,2,4,3:T(2,128)(2,1)} %bitcast.61) | data formatting | bytes 2534400 | tf_op jit(solution)/shard_map/all_to_all | solution.py:86
  267.6 7.9 %reshape.15 = bf16[704,900]{1,0:T(8,128)(2,1)S(1)} reshape(bf16[32,22,2,10,45]{4,3,2,1,0:T(8,128)(2,1)} %bitcast.63) | data formatting | bytes 2534400 | tf_op jit(solution)/shard_map/reshape | solution.py:90
  275.5 4.3 convolution_bitcast_fusion
  279.8 3.9 reshape.17
  283.7 2.5 fusion.2
  286.2 1.2 broadcast_multiply_fusion
  287.5 0.9 copy-done.3
  288.9 206.1 %all-reduce.2.cloned.1.call-done = f32[704,10,45]{0,2,1:T(8,128)} async-done(((f32[704,10,45]{0,2,1:T(8,128)}), f32[704,10,45]{0,2,1:T(8,128)}) %all-reduce.2.cloned.1.call-update) | async-done | bytes 1267216 | tf_op jit(solution)/shard_map/psum | solution.py:99
  495.0 1.2 bitcast_add_fusion
  496.2 8.1 %collective-permute-start = (f32[12,44,4]{1,2,0:T(4,128)S(1)}, f32[12,44,4]{1,2,0:T(4,128)S(1)}, u32[]{:S(2)}, u32[]{:S(2)}) collective-permute-start(f32[12,44,4]{1,2,0:T(4,128)S(1)} %get-tuple-element.26), channel_id=1, source_target_pairs={{0,1},{1,2},{2,3},{3,4},{4,5},{5,6},{6,7},{7,8},{8,9},{9,10},{10,1... | collective-permute-start | bytes 25352 | tf_op jit(solution)/shard_map/ppermute | solution.py:18
  504.4 10.1 %collective-permute-start.1 = (f32[12,44,4]{1,2,0:T(4,128)S(1)}, f32[12,44,4]{1,2,0:T(4,128)S(1)}, u32[]{:S(2)}, u32[]{:S(2)}) collective-permute-start(f32[12,44,4]{1,2,0:T(4,128)S(1)} %get-tuple-element.27), channel_id=1, source_target_pairs={{1,0},{2,1},{3,2},{4,3},{5,4},{6,5},{7,6},{8,7},{9,8},{10,9},{11,1... | collective-permute-start | bytes 25352 | tf_op jit(solution)/shard_map/ppermute | solution.py:19
  514.5 3.4 collective-permute-done.1
  518.2 4.9 collective-permute-start.2
  523.1 7.6 %collective-permute-start.3 = (f32[12,4,53]{1,2,0:T(8,128)S(1)}, f32[12,4,53]{1,2,0:T(8,128)S(1)}, u32[]{:S(2)}, u32[]{:S(2)}) collective-permute-start(f32[12,4,53]{1,2,0:T(8,128)S(1)} %get-tuple-element.25), channel_id=1, source_target_pairs={{32,0},{64,32},{96,64},{128,96},{160,128},{192,160},{224,192},{256... | collective-permute-start | bytes 30536 | tf_op jit(solution)/shard_map/ppermute | solution.py:19
  531.2 0.9 copy.49
  532.7 0.4 fusion.20
  533.1 0.4 fusion.12
  533.5 0.3 fusion.36
  534.2 0.9 copy.50
  (37 shorter events, 2.2 us)
Async XLA Ops:
  7.2 134.5 %copy-start = (bf16[2,10,22,1440]{3,0,2,1:T(2,128)(2,1)S(1)}, bf16[2,10,22,1440]{3,0,2,1:T(2,128)(2,1)}, u32[]{:S(2)}) copy-start(bf16[2,10,22,1440]{3,0,2,1:T(2,128)(2,1)} %param.7) | copy-start | bytes 3801604
  7.2 128.6 %all-gather.3.cloned.1.call-start = ((), (), s32[]{:S(2)}) async-start(), calls=%async_computation.3 | async-start | bytes 5013504 | tf_op jit(solution)/shard_map/all_gather | solution.py:83
  9.9 164.4 %all-to-all-start.1 = ((bf16[16,44,704]{2,1,0:T(8,128)(2,1)}), bf16[16,44,704]{2,1,0:T(8,128)(2,1)S(1)}, u32[]{:S(2)}, u32[]{:S(2)}) async-start(bf16[16,44,704]{2,1,0:T(8,128)(2,1)} %broadcast_in_dim.2), calls=%async_computation.1 | async-start | bytes 2359296 | tf_op jit(solution)/shard_map/all_to_all | solution.py:32
  174.3 1.0 copy-start.1
  175.3 59.7 %all-to-all-start = ((bf16[32,2,9900]{2,1,0:T(2,128)(2,1)}), bf16[32,2,9900]{2,1,0:T(2,128)(2,1)S(1)}, u32[]{:S(2)}, u32[]{:S(2)}) async-start(bf16[32,2,9900]{2,1,0:T(2,128)(2,1)} %reshape.22), calls=%async_computation | async-start | bytes 2555904 | tf_op jit(solution)/shard_map/all_to_all | solution.py:86
  187.8 307.2 %all-reduce.2.cloned.1.call-start = ((), (), s32[]{:S(2)}) async-start(), calls=%async_computation.2 | async-start | bytes 2949120 | tf_op jit(solution)/shard_map/psum | solution.py:99
  279.8 3.9 copy-start.2
  287.5 0.9 copy-start.3
  287.5 1.1 copy-start.4
  287.5 1.3 copy-start.5
  496.2 18.3 %collective-permute-start = (f32[12,44,4]{1,2,0:T(4,128)S(1)}, f32[12,44,4]{1,2,0:T(4,128)S(1)}, u32[]{:S(2)}, u32[]{:S(2)}) collective-permute-start(f32[12,44,4]{1,2,0:T(4,128)S(1)} %get-tuple-element.26), channel_id=1, source_target_pairs={{0,1},{1,2},{2,3},{3,4},{4,5},{5,6},{6,7},{7,8},{8,9},{9,10},{10,1... | collective-permute-start | bytes 25352 | tf_op jit(solution)/shard_map/ppermute | solution.py:18
  504.4 13.6 %collective-permute-start.1 = (f32[12,44,4]{1,2,0:T(4,128)S(1)}, f32[12,44,4]{1,2,0:T(4,128)S(1)}, u32[]{:S(2)}, u32[]{:S(2)}) collective-permute-start(f32[12,44,4]{1,2,0:T(4,128)S(1)} %get-tuple-element.27), channel_id=1, source_target_pairs={{1,0},{2,1},{3,2},{4,3},{5,4},{6,5},{7,6},{8,7},{9,8},{10,9},{11,1... | collective-permute-start | bytes 25352 | tf_op jit(solution)/shard_map/ppermute | solution.py:19
  518.2 13.9 %collective-permute-start.2 = (f32[12,4,53]{1,2,0:T(8,128)S(1)}, f32[12,4,53]{1,2,0:T(8,128)S(1)}, u32[]{:S(2)}, u32[]{:S(2)}) collective-permute-start(f32[12,4,53]{1,2,0:T(8,128)S(1)} %get-tuple-element.24), channel_id=1, source_target_pairs={{0,32},{32,64},{64,96},{96,128},{128,160},{160,192},{192,224},{224... | collective-permute-start | bytes 30536 | tf_op jit(solution)/shard_map/ppermute | solution.py:18
  523.1 8.9 %collective-permute-start.3 = (f32[12,4,53]{1,2,0:T(8,128)S(1)}, f32[12,4,53]{1,2,0:T(8,128)S(1)}, u32[]{:S(2)}, u32[]{:S(2)}) collective-permute-start(f32[12,4,53]{1,2,0:T(8,128)S(1)} %get-tuple-element.25), channel_id=1, source_target_pairs={{32,0},{64,32},{96,64},{128,96},{160,128},{192,160},{224,192},{256... | collective-permute-start | bytes 30536 | tf_op jit(solution)/shard_map/ppermute | solution.py:19
Sparse Core Ops, SparseCore 0:
  10.1 125.6 all-gather.2
  287.6 207.3 all-reduce.1
where the time goes:
time: 545 us; the launch traced here: 542 us
  waiting for transfers between devices  367 us (67%)
  local copies, waits for them, and re-layouts  86 us (16%)
  starting transfers between devices  57.4 us (11%)
  between operations  14.2 us (3%)
  matrix products  10.2 us (2%)
  other arithmetic  7.06 us (1%)
    psum x1, waiting for transfers between devices, per_device(): lax.psum(jnp.sum(localized * pert_rows.astype(jnp.float32), axis=1) * ens...  206 us
    all_gather x1, waiting for transfers between devices, per_device(): lax.all_gather(lon_loc, 'mem', axis=1, tiled=True)  112 us
    all_to_all x1, waiting for transfers between devices, per_device(): lax.all_to_all(along_lon, 'lat', split_axis=3, concat_axis=0, tiled=True)  44.9 us
    unnamed x20, local copies, waits for them, and re-layouts  28.6 us
    all_to_all x1, local copies, waits for them, and re-layouts, per_device(): lax.all_to_all(along_lon, 'lat', split_axis=3, concat_axis=0, tiled=True)  25.1 us
    ppermute x2, starting transfers between devices, padded_2(): after = lax.ppermute(leading, axis, down)  17.7 us
    convert_element_type x1, local copies, waits for them, and re-layouts, per_device(): along_lon = jnp.einsum('mfal,lc->amfc', control, lax.all_gather(lon_loc,...  15.6 us
    all_to_all x1, starting transfers between devices, sent_to_all(): lax.all_to_all(jnp.broadcast_to(shard[None], (length, *shard.shape)), axi...  14 us
  transfers between devices with their start and end apart: 8, of which 4 were waited for; matrix products, arithmetic and copies ran while one was open for 8% of the time, Pallas kernels for 0%

commit v1 on v0

--- a/solution.py
+++ b/solution.py
@@ -83,7 +83,10 @@
         lax.all_gather(lon_loc, "mem", axis=1, tiled=True),
         preferred_element_type=jnp.float32,
     ).astype(jnp.bfloat16)
-    banded = lax.all_to_all(along_lon, "lat", split_axis=3, concat_axis=0, tiled=True)
+    banded = jnp.concatenate(
+        lax.all_to_all(jnp.stack(jnp.split(along_lon, lax.axis_size("lat"), axis=3)), "lat", 0, 0),
+        axis=0,
+    )
     mem_here = banded.shape[1]
     fields = banded.shape[2]
     lon_width = banded.shape[3]

time: 545 us -> 512 us (0.939)
  local copies, waits for them, and re-layouts: 86 us -> 55.2 us
    all_to_all x1, local copies, waits for them, and re-layouts: 25.1 us -> 5.98 us  [per_device(): lax.all_to_all(jnp.stack(jnp.split(along_lon, lax.axis_size('lat'), axis=...]
    convert_element_type x1 -> x0, local copies, waits for them, and re-layouts: 15.6 us -> none  [per_device(): along_lon = jnp.einsum('mfal,lc->amfc', control, lax.all_gather(lon_loc,...]
    another operation x0 -> x3, local copies, waits for them, and re-layouts: none -> 12.5 us  [the longest x1 7.87 us: per_device(): flat_band = banded.reshape(banded.shape[0], mem_here * fields * lon_width)]
    psum x1, waiting for transfers between devices: 206 us -> 215 us  [per_device(): lax.psum(jnp.sum(localized * pert_rows.astype(jnp.float32), axis=1) * ens...]
    reshape x1 -> x0, local copies, waits for them, and re-layouts: 7.87 us -> none  [per_device(): flat_band = banded.reshape(banded.shape[0], mem_here * fields * lon_width)]
    all_to_all x1, waiting for transfers between devices: 44.9 us -> 37.5 us  [per_device(): lax.all_to_all(jnp.stack(jnp.split(along_lon, lax.axis_size('lat'), axis=...]
    unnamed x20 -> x51, local copies, waits for them, and re-layouts: 28.6 us -> 27.9 us
  transfers between devices with their start and end apart: 8 -> 8, of which waited for: 4 -> 4; matrix products, arithmetic and copies ran while one was open for 8% -> 7% of each run, Pallas kernels for 0% -> 0%
where the time goes in v1:
time: 512 us
  waiting for transfers between devices  368 us (72%)
  starting transfers between devices  57.5 us (11%)
  local copies, waits for them, and re-layouts  55.2 us (11%)
  between operations  14.5 us (3%)
  matrix products  9.08 us (2%)
  other arithmetic  7.2 us (1%)
    psum x1, waiting for transfers between devices, per_device(): lax.psum(jnp.sum(localized * pert_rows.astype(jnp.float32), axis=1) * ens...  215 us
    all_gather x1, waiting for transfers between devices, per_device(): lax.all_gather(lon_loc, 'mem', axis=1, tiled=True)  112 us
    all_to_all x1, waiting for transfers between devices, per_device(): lax.all_to_all(jnp.stack(jnp.split(along_lon, lax.axis_size('lat'), axis=...  37.5 us
    unnamed x51, local copies, waits for them, and re-layouts  27.9 us
    ppermute x2, starting transfers between devices, padded_2(): after = lax.ppermute(leading, axis, down)  17.7 us
    all_to_all x1, starting transfers between devices, sent_to_all(): lax.all_to_all(jnp.broadcast_to(shard[None], (length, *shard.shape)), axi...  14 us
    ppermute x2, starting transfers between devices, padded_2(): before = lax.ppermute(last, axis, up)  13.1 us
    all_to_all x1, starting transfers between devices, per_device(): lax.all_to_all(jnp.stack(jnp.split(along_lon, lax.axis_size('lat'), axis=...  12.5 us
  transfers between devices with their start and end apart: 8, of which 4 were waited for; matrix products, arithmetic and copies ran while one was open for 7% of the time, Pallas kernels for 0%

profile of v1, /device:TPU:1, one launch (start us, length us, event | category | flops | bytes accessed | tf_op | source)
XLA Modules:
  0.0 511.6 jit_solution(5111320219431952085)
XLA Ops:
  7.2 0.7 all-gather.3.cloned.1.call-update
  7.9 2.0 broadcast_in_dim.2
  9.9 14.0 %all-to-all-start.1 = ((bf16[16,44,704]{2,1,0:T(8,128)(2,1)}), bf16[16,44,704]{2,1,0:T(8,128)(2,1)S(1)}, u32[]{:S(2)}, u32[]{:S(2)}) async-start(bf16[16,44,704]{2,1,0:T(8,128)(2,1)} %broadcast_in_dim.2), calls=%async_computation.1 | async-start | bytes 2359296 | tf_op jit(solution)/shard_map/all_to_all | solution.py:32
  23.9 111.8 %all-gather.3.cloned.1.call-done = bf16[16,90,1440]{2,1,0:T(8,128)(2,1)} async-done(((bf16[1,90,1440]{2,1,0:T(8,128)(2,1)}), bf16[16,90,1440]{2,1,0:T(8,128)(2,1)}) %all-gather.3.cloned.1.call-update) | async-done | bytes 4147216 | tf_op jit(solution)/shard_map/all_gather | solution.py:83
  135.7 5.9 %reshape.15 = bf16[1440,1440,1,1]{1,0,2,3:T(8,128)(2,1)} reshape(bf16[16,90,1440]{2,1,0:T(8,128)(2,1)} %all-gather.3.cloned.1.call-done) | data formatting | bytes 8294400
  141.7 4.8 fusion.6
  150.5 4.5 copy.44
  155.0 9.7 %reshape.17 = bf16[32,2,9900]{2,1,0:T(2,128)(2,1)} reshape(bf16[32,22,10,2,45]{4,3,2,1,0:T(2,128)(2,1)} %bitcast.188) | data formatting | bytes 2534400
  164.7 1.0 copy-done.1
  165.7 12.5 %all-to-all-start = ((bf16[32,2,9900]{2,1,0:T(2,128)(2,1)}), bf16[32,2,9900]{2,1,0:T(2,128)(2,1)S(1)}, u32[]{:S(2)}, u32[]{:S(2)}) async-start(bf16[32,2,9900]{2,1,0:T(2,128)(2,1)} %reshape.17), calls=%async_computation | async-start | bytes 2555904 | tf_op jit(solution)/shard_map/all_to_all | solution.py:87
  178.4 2.3 reshape.11
  180.8 37.5 %all-to-all-done = bf16[32,2,9900]{2,1,0:T(2,128)(2,1)S(1)} async-done(((bf16[32,2,9900]{2,1,0:T(2,128)(2,1)}), bf16[32,2,9900]{2,1,0:T(2,128)(2,1)S(1)}, u32[]{:S(2)}, u32[]{:S(2)}) %all-to-all-start) | async-done | bytes 1267232 | tf_op jit(solution)/shard_map/all_to_all | solution.py:87
  218.2 5.4 %reshape.18 = bf16[32,22,10,2,45]{4,3,2,1,0:T(2,128)(2,1)} reshape(bf16[32,2,9900]{2,1,0:T(2,128)(2,1)S(1)} %all-to-all-done) | data formatting | bytes 2534400
  223.6 6.0 %copy.20 = bf16[32,22,2,10,45]{4,3,2,1,0:T(8,128)(2,1)} copy(bf16[32,22,2,10,45]{4,2,3,1,0:T(2,128)(2,1)} %bitcast.189) | data formatting | bytes 2534400 | tf_op jit(solution)/shard_map/all_to_all | solution.py:87
  229.6 7.9 %reshape_reshape.3 = bf16[704,900]{1,0:T(8,128)(2,1)S(1)} reshape(bf16[32,22,2,10,45]{4,3,2,1,0:T(8,128)(2,1)} %copy.20) | data formatting | bytes 2534400 | tf_op jit(solution)/shard_map/reshape;reshape | solution.py:93
  237.4 4.3 convolution_bitcast_fusion
  241.7 3.9 reshape.12
  245.7 2.7 fusion.2
  248.4 1.2 broadcast_multiply_fusion
  250.1 214.7 %all-reduce.2.cloned.1.call-done = f32[704,10,45]{0,2,1:T(8,128)} async-done(((f32[704,10,45]{0,2,1:T(8,128)}), f32[704,10,45]{0,2,1:T(8,128)}) %all-reduce.2.cloned.1.call-update) | async-done | bytes 1267216 | tf_op jit(solution)/shard_map/psum | solution.py:102
  464.8 1.2 bitcast_add_fusion
  466.0 8.1 %collective-permute-start = (f32[12,44,4]{1,2,0:T(4,128)S(1)}, f32[12,44,4]{1,2,0:T(4,128)S(1)}, u32[]{:S(2)}, u32[]{:S(2)}) collective-permute-start(f32[12,44,4]{1,2,0:T(4,128)S(1)} %get-tuple-element.24), channel_id=1, source_target_pairs={{0,1},{1,2},{2,3},{3,4},{4,5},{5,6},{6,7},{7,8},{8,9},{9,10},{10,1... | collective-permute-start | bytes 25352 | tf_op jit(solution)/shard_map/ppermute | solution.py:18
  474.1 10.1 %collective-permute-start.1 = (f32[12,44,4]{1,2,0:T(4,128)S(1)}, f32[12,44,4]{1,2,0:T(4,128)S(1)}, u32[]{:S(2)}, u32[]{:S(2)}) collective-permute-start(f32[12,44,4]{1,2,0:T(4,128)S(1)} %get-tuple-element.25), channel_id=1, source_target_pairs={{1,0},{2,1},{3,2},{4,3},{5,4},{6,5},{7,6},{8,7},{9,8},{10,9},{11,1... | collective-permute-start | bytes 25352 | tf_op jit(solution)/shard_map/ppermute | solution.py:19
  484.3 3.4 collective-permute-done.1
  487.9 4.9 collective-permute-start.2
  492.9 7.6 %collective-permute-start.3 = (f32[12,4,53]{1,2,0:T(8,128)S(1)}, f32[12,4,53]{1,2,0:T(8,128)S(1)}, u32[]{:S(2)}, u32[]{:S(2)}) collective-permute-start(f32[12,4,53]{1,2,0:T(8,128)S(1)} %get-tuple-element.23), channel_id=1, source_target_pairs={{32,0},{64,32},{96,64},{128,96},{160,128},{192,160},{224,192},{256... | collective-permute-start | bytes 30536 | tf_op jit(solution)/shard_map/ppermute | solution.py:19
  500.9 0.9 copy.31
  502.5 0.4 fusion.20
  502.9 0.4 fusion.12
  503.2 0.3 fusion.36
  503.6 0.3 fusion.28
  503.9 0.9 copy.32
  (69 shorter events, 5.9 us)
Async XLA Ops:
  7.2 134.5 %copy-start = (bf16[2,10,22,1440]{3,0,2,1:T(2,128)(2,1)S(1)}, bf16[2,10,22,1440]{3,0,2,1:T(2,128)(2,1)}, u32[]{:S(2)}) copy-start(bf16[2,10,22,1440]{3,0,2,1:T(2,128)(2,1)} %param.7) | copy-start | bytes 3801604
  7.2 128.6 %all-gather.3.cloned.1.call-start = ((), (), s32[]{:S(2)}) async-start(), calls=%async_computation.3 | async-start | bytes 5013504 | tf_op jit(solution)/shard_map/all_gather | solution.py:83
  9.9 154.8 %all-to-all-start.1 = ((bf16[16,44,704]{2,1,0:T(8,128)(2,1)}), bf16[16,44,704]{2,1,0:T(8,128)(2,1)S(1)}, u32[]{:S(2)}, u32[]{:S(2)}) async-start(bf16[16,44,704]{2,1,0:T(8,128)(2,1)} %broadcast_in_dim.2), calls=%async_computation.1 | async-start | bytes 2359296 | tf_op jit(solution)/shard_map/all_to_all | solution.py:32
  164.7 1.0 copy-start.1
  165.7 52.5 %all-to-all-start = ((bf16[32,2,9900]{2,1,0:T(2,128)(2,1)}), bf16[32,2,9900]{2,1,0:T(2,128)(2,1)S(1)}, u32[]{:S(2)}, u32[]{:S(2)}) async-start(bf16[32,2,9900]{2,1,0:T(2,128)(2,1)} %reshape.17), calls=%async_computation | async-start | bytes 2555904 | tf_op jit(solution)/shard_map/all_to_all | solution.py:87
  178.2 286.6 %all-reduce.2.cloned.1.call-start = ((), (), s32[]{:S(2)}) async-start(), calls=%async_computation.2 | async-start | bytes 2949120 | tf_op jit(solution)/shard_map/psum | solution.py:102
  241.7 3.9 copy-start.2
  245.7 4.0 copy-start.3
  245.7 4.2 copy-start.4
  248.3 1.7 copy-start.5
  466.0 18.3 %collective-permute-start = (f32[12,44,4]{1,2,0:T(4,128)S(1)}, f32[12,44,4]{1,2,0:T(4,128)S(1)}, u32[]{:S(2)}, u32[]{:S(2)}) collective-permute-start(f32[12,44,4]{1,2,0:T(4,128)S(1)} %get-tuple-element.24), channel_id=1, source_target_pairs={{0,1},{1,2},{2,3},{3,4},{4,5},{5,6},{6,7},{7,8},{8,9},{9,10},{10,1... | collective-permute-start | bytes 25352 | tf_op jit(solution)/shard_map/ppermute | solution.py:18
  474.1 13.6 %collective-permute-start.1 = (f32[12,44,4]{1,2,0:T(4,128)S(1)}, f32[12,44,4]{1,2,0:T(4,128)S(1)}, u32[]{:S(2)}, u32[]{:S(2)}) collective-permute-start(f32[12,44,4]{1,2,0:T(4,128)S(1)} %get-tuple-element.25), channel_id=1, source_target_pairs={{1,0},{2,1},{3,2},{4,3},{5,4},{6,5},{7,6},{8,7},{9,8},{10,9},{11,1... | collective-permute-start | bytes 25352 | tf_op jit(solution)/shard_map/ppermute | solution.py:19
  487.9 13.9 %collective-permute-start.2 = (f32[12,4,53]{1,2,0:T(8,128)S(1)}, f32[12,4,53]{1,2,0:T(8,128)S(1)}, u32[]{:S(2)}, u32[]{:S(2)}) collective-permute-start(f32[12,4,53]{1,2,0:T(8,128)S(1)} %get-tuple-element.22), channel_id=1, source_target_pairs={{0,32},{32,64},{64,96},{96,128},{128,160},{160,192},{192,224},{224... | collective-permute-start | bytes 30536 | tf_op jit(solution)/shard_map/ppermute | solution.py:18
  492.9 8.9 %collective-permute-start.3 = (f32[12,4,53]{1,2,0:T(8,128)S(1)}, f32[12,4,53]{1,2,0:T(8,128)S(1)}, u32[]{:S(2)}, u32[]{:S(2)}) collective-permute-start(f32[12,4,53]{1,2,0:T(8,128)S(1)} %get-tuple-element.23), channel_id=1, source_target_pairs={{32,0},{64,32},{96,64},{128,96},{160,128},{192,160},{224,192},{256... | collective-permute-start | bytes 30536 | tf_op jit(solution)/shard_map/ppermute | solution.py:19
Sparse Core Ops, SparseCore 0:
  10.1 125.6 all-gather.2
  249.8 214.9 all-reduce.1
